TPU v7x, 32 devices: a whole 2x2x4 slice. The times are simulated.
32 devices in a mesh: dp: 2 (over x), fsdp: 4 (over z), expert: 4 (over y, core).
Axes of the slice: x: 2, y: 2, z: 4, core: 2. Of those that a mesh axis runs over, the one named last changes fastest.
Arguments:
- window: bfloat16 [256, 4096], P('fsdp'), may hold values from -3 to 3
- attention_gain: float32 [4096], replicated, may hold values from 0.1 to 1.9
- query_weight: bfloat16 [4096, 4096], P('fsdp', 'expert'), may hold values from -0.09375 to 0.09375
- key_weight: bfloat16 [4096, 1024], P('fsdp', 'expert'), may hold values from -0.1875 to 0.1875
- value_weight: bfloat16 [4096, 1024], P('fsdp', 'expert'), may hold values from -0.1875 to 0.1875
- out_weight: bfloat16 [4096, 4096], P('expert', 'fsdp'), may hold values from -0.1875 to 0.1875
- cache_keys: bfloat16 [1024, 1024], P('dp', 'expert'), may hold values from -104 to 104
- cache_values: bfloat16 [1024, 1024], P('dp', 'expert'), may hold values from -12 to 12
- occluded: int32 [1024, 2], P('dp'), may hold values from 0 to 1, as said below
- feedforward_gain: float32 [4096], replicated, may hold values from 0.1 to 1.9
- router_weight: bfloat16 [4096, 4], replicated, may hold values from -0.0234375 to 0.0234375
- chosen_experts: int32 [2, 256, 2], P('dp', 'fsdp'), may hold values from 0 to 3, all different within a row; in each aligned block of 64 rows (0 to 63, 64 to 127, ..., all dimensions but the last counted through in order) at most 64 rows name the same one
- gate_weight: bfloat16 [4, 12288, 4096], P('expert', ('dp', 'fsdp')), may hold values from -0.09375 to 0.09375
- up_weight: bfloat16 [4, 12288, 4096], P('expert', ('dp', 'fsdp')), may hold values from -0.09375 to 0.09375
- down_weight: bfloat16 [4, 12288, 4096], P('expert', ('dp', 'fsdp')), may hold values from -0.0546875 to 0.0546875
Outputs:
- layer_output: bfloat16 [2, 256, 4096], P('dp', 'fsdp')
Inputs may be any that keep to these rules, and one draw needn't show every extreme that they name: `chosen_experts`: each row names 2 different experts. In each aligned block of 64 rows, counting the leading dimensions together (the rows of one device), no expert is named by more than 64 rows, a bound that some block reaches. `occluded`: constant over each aligned run of 64 prefix positions.
All inputs are finite; a program needn't handle non-finite values.
Results may differ from a plain program's by a relative error of at most 0.0095.
The roundings to bfloat16 on the way count: a program that leaves them out, or rounds other values in their place, can miss the bound.
Values may be sent and summed in bfloat16 or wider, within the bound.
A program may use at most 128 MiB of HBM per device.

v0:
```python
import jax
import jax.numpy as jnp
from jax import lax
from jax.sharding import PartitionSpec as P

HD = 128
TOP = 2
epsilon = 1e-05
rope_base = 1000000.0
floor_score = -1e30


def rms_norm(values, scales):
    widened = values.astype(jnp.float32)
    inverse = lax.rsqrt(jnp.mean(widened * widened, axis=-1, keepdims=True) + epsilon)
    return (widened * inverse * scales).astype(jnp.bfloat16)


def rotate(vectors, positions):
    halfway = vectors.shape[-1] // 2
    powers = jnp.arange(halfway, dtype=jnp.float32) * (2.0 / vectors.shape[-1])
    frequency = rope_base ** (-powers)
    angles = positions.astype(jnp.float32)[:, None] * frequency[None, :]
    cosine = jnp.cos(angles)[:, None, :]
    sine_part = jnp.sin(angles)[:, None, :]
    former = vectors[..., :halfway]
    latter = vectors[..., halfway:]
    return jnp.concatenate(
        [former * cosine - latter * sine_part, latter * cosine + former * sine_part], axis=-1
    )


def absorb_block(running, scores, visible, values_block):
    running_top, running_total, running_output = running
    masked = jnp.where(visible, scores, floor_score)
    fresh_top = jnp.maximum(running_top, jnp.max(masked, axis=-1))
    weights = jnp.where(visible, jnp.exp(masked - fresh_top[..., None]), 0.0)
    fresh_total = jnp.sum(weights, axis=-1)
    fresh_output = jnp.einsum(
        "kgtn,nkd->kgtd",
        weights.astype(jnp.bfloat16),
        values_block,
        preferred_element_type=jnp.float32,
    )
    return (fresh_top, fresh_total, fresh_output)


def local(
    window,
    attention_gain,
    query_weight,
    key_weight,
    value_weight,
    out_weight,
    cache_keys,
    cache_values,
    occluded,
    feedforward_gain,
    router_weight,
    chosen_experts,
    gate_weight,
    up_weight,
    down_weight,
):
    token_rows = window.shape[0]
    fsdp_count = lax.axis_size("fsdp")
    fsdp_place = lax.axis_index("fsdp")
    data_place = lax.axis_index("dp")
    expert_place = lax.axis_index("expert")
    query_heads = query_weight.shape[1] // HD
    key_heads = key_weight.shape[1] // HD
    grouping = query_heads // key_heads
    window_rows = token_rows * fsdp_count
    prefix_rows = cache_keys.shape[0] * lax.axis_size("dp")
    score_scale = HD ** (-0.5)
    normed = rms_norm(window, attention_gain)
    first_row = fsdp_place * token_rows
    own_positions = prefix_rows + first_row + jnp.arange(token_rows, dtype=jnp.int32)
    all_positions = prefix_rows + jnp.arange(window_rows, dtype=jnp.int32)
    everyone = lax.all_gather(normed, "fsdp", axis=0, tiled=True)
    slab_width = query_weight.shape[0]
    columns = lax.dynamic_slice_in_dim(everyone, fsdp_place * slab_width, slab_width, 1)
    row_block = columns
    query_sum = lax.psum_scatter(
        jnp.dot(row_block, query_weight, preferred_element_type=jnp.float32),
        "fsdp",
        scatter_dimension=0,
        tiled=True,
    )
    key_sum, value_sum = lax.psum(
        (
            jnp.dot(columns, key_weight, preferred_element_type=jnp.float32),
            jnp.dot(columns, value_weight, preferred_element_type=jnp.float32),
        ),
        "fsdp",
    )
    queries = rotate(query_sum.reshape(token_rows, query_heads, HD), own_positions).astype(
        jnp.bfloat16
    )
    window_keys = (
        rotate(key_sum.reshape(window_rows, key_heads, HD), all_positions)
        .astype(jnp.bfloat16)
        .reshape(window_rows, key_heads * HD)
    )
    window_values = value_sum.astype(jnp.bfloat16)
    query_grid = queries.reshape(token_rows, key_heads, grouping, HD)
    fresh_keys = window_keys.reshape(window_rows, key_heads, HD)
    fresh_values = window_values.reshape(window_rows, key_heads, HD)
    window_scores = (
        jnp.einsum("tkgd,nkd->kgtn", query_grid, fresh_keys, preferred_element_type=jnp.float32)
        * score_scale
    )
    causal = jnp.arange(window_rows)[None, :] <= (first_row + jnp.arange(token_rows))[:, None]
    empty_state = (
        jnp.full((key_heads, grouping, token_rows), floor_score, jnp.float32),
        jnp.zeros((key_heads, grouping, token_rows), jnp.float32),
        jnp.zeros((key_heads, grouping, token_rows, HD), jnp.float32),
    )
    window_state = absorb_block(empty_state, window_scores, causal, fresh_values)
    occluded_flags = occluded.astype(jnp.bfloat16)
    keys_block = lax.all_gather(cache_keys, "dp", axis=0, tiled=True)
    values_block = lax.all_gather(cache_values, "dp", axis=0, tiled=True)
    flags_block = lax.all_gather(occluded_flags, "dp", axis=0, tiled=True)
    block_length = keys_block.shape[0]
    scores = (
        jnp.einsum(
            "tkgd,nkd->kgtn",
            query_grid,
            keys_block.reshape(block_length, key_heads, HD),
            preferred_element_type=jnp.float32,
        )
        * score_scale
    )
    visible = lax.dynamic_slice_in_dim(flags_block, data_place, 1, 1)[:, 0] == 0
    prefix_state = absorb_block(
        empty_state, scores, visible, values_block.reshape(block_length, key_heads, HD)
    )
    overall = jnp.maximum(prefix_state[0], window_state[0])
    prefix_fade = jnp.exp(prefix_state[0] - overall)
    window_fade = jnp.exp(window_state[0] - overall)
    denominator = prefix_state[1] * prefix_fade + window_state[1] * window_fade
    head_values = (
        prefix_state[2] * prefix_fade[..., None] + window_state[2] * window_fade[..., None]
    ) / denominator[..., None]
    attended = (
        head_values.transpose(2, 0, 1, 3).reshape(token_rows, query_heads * HD).astype(jnp.bfloat16)
    )
    head_terms = jnp.dot(
        attended,
        lax.all_gather(out_weight, "fsdp", axis=1, tiled=True),
        preferred_element_type=jnp.float32,
    )
    residual = window.astype(jnp.float32) + lax.psum(head_terms, "expert")
    normed_mix = rms_norm(residual, feedforward_gain)
    logits = jnp.dot(normed_mix, router_weight, preferred_element_type=jnp.float32)
    expert_count = router_weight.shape[1]
    expert_picks = chosen_experts.reshape(token_rows, TOP)
    matches = expert_picks[:, :, None] == jnp.arange(expert_count, dtype=jnp.int32)[None, None, :]
    picked = jnp.sum(jnp.where(matches, logits[:, None, :], 0.0), axis=-1)
    gate_shares = jax.nn.sigmoid(picked - picked[:, ::-1])
    expert_hits = expert_picks == expert_place
    taken_flag = jnp.any(expert_hits, axis=1).astype(jnp.int32)
    weight_mine = jnp.sum(jnp.where(expert_hits, gate_shares, 0.0), axis=1)
    capacity = min(token_rows, 2 * token_rows * TOP // expert_count)
    slot_numbers = jnp.cumsum(taken_flag) - taken_flag
    placing = (slot_numbers[:, None] == jnp.arange(capacity, dtype=jnp.int32)[None, :]) & (
        taken_flag[:, None] == 1
    )
    send_rows = lax.dot_general(
        placing.astype(jnp.bfloat16),
        normed_mix,
        (((0,), (0,)), ((), ())),
        preferred_element_type=jnp.float32,
    ).astype(jnp.bfloat16)
    gate_rows = gate_weight[0]
    up_rows = up_weight[0]
    down_rows = down_weight[0]
    contract_last = (((1,), (1,)), ((), ()))
    piece_rows = lax.all_gather(send_rows, ("dp", "fsdp"), axis=0, tiled=True)
    gate_values = lax.dot_general(
        piece_rows, gate_rows, contract_last, preferred_element_type=jnp.float32
    )
    lifted = lax.dot_general(piece_rows, up_rows, contract_last, preferred_element_type=jnp.float32)
    hidden = (jax.nn.silu(gate_values) * lifted).astype(jnp.bfloat16)
    row_block = hidden
    expert_output = lax.psum_scatter(
        jnp.dot(row_block, down_rows, preferred_element_type=jnp.float32).astype(jnp.bfloat16),
        ("dp", "fsdp"),
        scatter_dimension=0,
        tiled=True,
    ).astype(jnp.float32)
    returned = jnp.dot(
        placing.astype(jnp.float32),
        expert_output,
        precision=lax.Precision.HIGHEST,
        preferred_element_type=jnp.float32,
    )
    mixture = lax.psum(returned * weight_mine[:, None], "expert")
    return (residual + mixture).astype(jnp.bfloat16).reshape(1, token_rows, residual.shape[1])


def solution(mesh):
    placed = (
        P("fsdp", None),
        P(),
        P("fsdp", "expert"),
        P("fsdp", "expert"),
        P("fsdp", "expert"),
        P("expert", "fsdp"),
        P("dp", "expert"),
        P("dp", "expert"),
        P("dp", None),
        P(),
        P(),
        P("dp", "fsdp", None),
        P("expert", ("dp", "fsdp"), None),
        P("expert", ("dp", "fsdp"), None),
        P("expert", ("dp", "fsdp"), None),
    )
    return jax.shard_map(
        local, mesh=mesh, in_specs=placed, out_specs=P("dp", "fsdp", None), check_vma=False
    )
```

profile of v0, /device:TPU:0, one launch (start us, length us, event | category | flops | bytes accessed | tf_op | source)
XLA Modules:
  0.0 560.7 jit_solution(14526967308801473713)
XLA Ops:
  6.5 1.4 fusion.29
  8.0 2.0 fusion.31
  10.0 0.0 all-gather.4.cloned.1.call-update
  10.0 0.0 all-reduce.5.cloned.1.call-start
  10.1 48.7 %all-gather.4.cloned.1.call-done = bf16[256,4096]{1,0:T(8,128)(2,1)} async-done(((bf16[64,4096]{1,0:T(8,128)(2,1)}), bf16[256,4096]{1,0:T(8,128)(2,1)}) %all-gather.4.cloned.1.call-update) | async-done | bytes 2097168 | tf_op jit(solution)/shard_map/all_gather | solution.py:80
  58.8 1.4 fusion.43
  60.2 0.8 copy.41
  61.0 0.0 all-reduce.5.cloned.1.call-update
  61.1 0.0 reduce-scatter.3.cloned.1.call-start
  61.1 2.7 fusion.45
  63.9 0.0 reduce-scatter.3.cloned.1.call-update
  63.9 0.0 all-gather.6.cloned.1.call-start
  63.9 0.5 all-gather.6.cloned.1.call-update
  64.5 0.0 all-reduce.7.cloned.1.call-start
  64.5 0.0 copy-done.11
  64.6 0.3 copy-done.6
  64.8 0.1 copy.37
  65.0 0.1 copy.39
  65.1 4.3 all_gather.18
  69.5 7.9 %all_gather.20 = bf16[1024,256]{0,1:T(8,128)(2,1)S(1)} all-gather(bf16[512,256]{0,1:T(8,128)(2,1)S(1)} %copy.37), channel_id=1, replica_groups=mesh['dp'=2,'fsdp'=4,'expert'=4] {'dp'}, dimensions={0}, use_global_device_ids=true | all-gather | bytes 786432 | tf_op jit(solution)/shard_map/all_gather | solution.py:121
  77.4 7.1 %all_gather.21 = bf16[1024,256]{0,1:T(8,128)(2,1)S(1)} all-gather(bf16[512,256]{0,1:T(8,128)(2,1)S(1)} %copy.39), channel_id=1, replica_groups=mesh['dp'=2,'fsdp'=4,'expert'=4] {'dp'}, dimensions={0}, use_global_device_ids=true | all-gather | bytes 786432 | tf_op jit(solution)/shard_map/all_gather | solution.py:122
  84.5 0.1 iota_compare_fusion
  84.6 0.2 multiply_cosine_fusion.1
  84.8 0.5 multiply_cosine_fusion
  85.3 1.3 fusion.41
  86.7 23.1 %all-reduce.10 = bf16[256,256]{1,0:T(8,128)(2,1)S(1)} all-reduce(f32[256,256]{1,0:T(8,128)S(1)} %fusion.41), channel_id=1, replica_groups=mesh['dp'=2,'fsdp'=4,'expert'=4] {'fsdp'}, use_global_device_ids=true, to_apply=%region_5.6 | all-reduce | flops 65536 | bytes 393216 | tf_op jit(solution)/shard_map/psum | solution.py:90
  109.9 0.0 all-reduce.5.cloned.1.call-done
  109.9 1.2 subtract_convert_fusion
  111.1 14.3 %reduce-scatter.3.cloned.1.call-done = f32[64,1024]{1,0:T(8,128)} async-done(((f32[256,1024]{1,0:T(8,128)}), f32[64,1024]{1,0:T(8,128)}) %reduce-scatter.3.cloned.1.call-update) | async-done | bytes 262160 | tf_op jit(solution)/shard_map/reduce_scatter | solution.py:84
  125.4 1.0 copy.55
  126.4 0.2 subtract_convert_fusion.1
  126.6 0.4 fusion.79
  127.1 0.3 fusion.39
  127.3 0.6 bitcast_reduce_fusion
  127.9 0.6 fusion.20
  128.6 0.6 fusion.27
  129.2 0.3 fusion.28
  129.5 0.1 copy.43
  129.7 0.1 convert_element_type.96
  129.8 145.4 %all-gather.6.cloned.1.call-done = bf16[1024,4096]{1,0:T(8,128)(2,1)} async-done(((bf16[1024,1024]{1,0:T(8,128)(2,1)}), bf16[1024,4096]{1,0:T(8,128)(2,1)}) %all-gather.6.cloned.1.call-update) | async-done | bytes 8388624 | tf_op jit(solution)/shard_map/all_gather | solution.py:150
  275.1 6.0 %fusion.80 = f32[64,4096]{1,0:T(8,128)} fusion(bf16[64,1024]{1,0:T(8,128)(2,1)S(1)} %convert_element_type.96, bf16[1024,4096]{1,0:T(8,128)(2,1)} %all-gather.6.cloned.1.call-done), kind=kOutput, calls=%fused_computation.113 | convolution fusion | flops 536870912 | bytes 9568256 | tf_op jit(solution)/shard_map/dot_general | solution.py:148
  281.2 0.0 all-reduce.7.cloned.1.call-update
  281.2 0.0 all-gather.8.cloned.1.call-start
  281.3 0.1 copy.44
  281.4 0.1 reduce-window.8
  281.5 0.1 reduce.1
  281.6 34.0 %all-reduce.7.cloned.1.call-done = f32[64,4096]{1,0:T(8,128)} async-done(((f32[64,4096]{1,0:T(8,128)}), f32[64,4096]{1,0:T(8,128)}) %all-reduce.7.cloned.1.call-update) | async-done | bytes 1048592 | tf_op jit(solution)/shard_map/psum | solution.py:153
  315.6 1.6 multiply_reduce_fusion
  317.2 0.2 multiply_convert_fusion
  317.4 1.2 convolution_convert_fusion
  318.6 0.0 all-gather.8.cloned.1.call-update
  318.7 0.2 reduce-scatter.5.cloned.1.call-start
  318.9 73.7 %all-gather.8.cloned.1.call-done = bf16[512,4096]{1,0:T(8,128)(2,1)} async-done(((bf16[64,4096]{1,0:T(8,128)(2,1)}), bf16[512,4096]{1,0:T(8,128)(2,1)}) %all-gather.8.cloned.1.call-update) | async-done | bytes 4194320 | tf_op jit(solution)/shard_map/all_gather | solution.py:179
  392.6 12.1 %fusion.4 = f32[512,1536]{1,0:T(8,128)} fusion(bf16[512,4096]{1,0:T(8,128)(2,1)} %all-gather.8.cloned.1.call-done, bf16[1,1536,4096]{2,1,0:T(8,128)(2,1)} %param.27), kind=kOutput, calls=%fused_computation.4 | convolution fusion | flops 6442450944 | bytes 19922944 | tf_op jit(solution)/shard_map/dot_general | solution.py:180
  404.7 21.8 %fusion.6 = bf16[512,4096]{1,0:T(8,128)(2,1)} fusion(bf16[1,1536,4096]{2,1,0:T(8,128)(2,1)} %param.29, bf16[512,4096]{1,0:T(8,128)(2,1)} %all-gather.8.cloned.1.call-done, bf16[1,1536,4096]{2,1,0:T(8,128)(2,1)} %param.28, f32[512,1536]{1,0:T(8,128)} %fusion.4), kind=kOutput, calls=%fused_computation.6 | convolution fusion | flops 12891717632 | bytes 36700160 | tf_op jit(solution)/shard_map/dot_general | solution.py:187
  426.5 0.0 reduce-scatter.5.cloned.1.call-update
  426.5 0.0 all-reduce.9.cloned.1.call-start
  426.6 0.7 copy-done.8
  427.3 0.2 fusion.81
  427.6 85.3 %reduce-scatter.5.cloned.1.call-done = bf16[64,4096]{1,0:T(8,128)(2,1)} async-done(((bf16[512,4096]{1,0:T(8,128)(2,1)}), bf16[64,4096]{1,0:T(8,128)(2,1)}) %reduce-scatter.5.cloned.1.call-update) | async-done | bytes 524304 | tf_op jit(solution)/shard_map/reduce_scatter | solution.py:186
  512.9 2.4 convolution_multiply_fusion
  515.3 0.0 all-reduce.9.cloned.1.call-update
  515.4 36.0 %all-reduce.9.cloned.1.call-done = f32[64,4096]{1,0:T(8,128)} async-done(((f32[64,4096]{1,0:T(8,128)}), f32[64,4096]{1,0:T(8,128)}) %all-reduce.9.cloned.1.call-update) | async-done | bytes 1048592 | tf_op jit(solution)/shard_map/psum | solution.py:198
  551.3 2.5 fusion.38
  (42 shorter events, 0.3 us)
Async XLA Ops:
  6.5 54.6 %copy-start = (bf16[1024,1024]{1,0:T(8,128)(2,1)S(1)}, bf16[1024,1024]{1,0:T(8,128)(2,1)}, u32[]{:S(2)}) copy-start(bf16[1024,1024]{1,0:T(8,128)(2,1)} %param.17) | copy-start | bytes 6291460
  6.5 52.3 %copy-start.4 = (bf16[1024,256]{1,0:T(8,128)(2,1)S(1)}, bf16[1024,256]{1,0:T(8,128)(2,1)}, u32[]{:S(2)}) copy-start(bf16[1024,256]{1,0:T(8,128)(2,1)} %param.18) | copy-start | bytes 1572868
  6.5 52.3 %all-gather.4.cloned.1.call-start = ((), (), s32[]{:S(2)}) async-start(), calls=%async_computation.2 | async-start | bytes 2621440 | tf_op jit(solution)/shard_map/all_gather | solution.py:80
  10.0 99.9 %all-reduce.5.cloned.1.call-start = ((), (), s32[]{:S(2)}) async-start(), calls=%async_computation.4 | async-start | bytes 524288 | tf_op jit(solution)/shard_map/psum | solution.py:90
  61.1 64.4 %reduce-scatter.3.cloned.1.call-start = ((), (), s32[]{:S(2)}) async-start(), calls=%async_computation.3 | async-start | bytes 1310720 | tf_op jit(solution)/shard_map/reduce_scatter | solution.py:84
  63.9 0.7 copy-start.11
  63.9 1.0 copy-start.6
  63.9 1.1 copy-start.7
  63.9 21.4 %copy-start.5 = (bf16[1024,256]{1,0:T(8,128)(2,1)S(1)}, bf16[1024,256]{1,0:T(8,128)(2,1)}, u32[]{:S(2)}) copy-start(bf16[1024,256]{1,0:T(8,128)(2,1)} %param.19) | copy-start | bytes 1572868
  63.9 211.2 %all-gather.6.cloned.1.call-start = ((), (), s32[]{:S(2)}) async-start(), calls=%async_computation.5 | async-start | bytes 10485760 | tf_op jit(solution)/shard_map/all_gather | solution.py:150
  64.5 251.1 %all-reduce.7.cloned.1.call-start = ((), (), s32[]{:S(2)}) async-start(), calls=%async_computation.6 | async-start | bytes 2097152 | tf_op jit(solution)/shard_map/psum | solution.py:153
  129.7 151.5 %copy-start.10 = (s32[1,64,2]{1,2,0:T(2,128)S(1)}, s32[1,64,2]{1,2,0:T(2,128)}, u32[]{:S(2)}) copy-start(s32[1,64,2]{1,2,0:T(2,128)} %param.26) | copy-start | bytes 1540
  129.7 185.9 %copy-start.2 = (bf16[64,4096]{1,0:T(8,128)(2,1)S(1)}, bf16[64,4096]{1,0:T(8,128)(2,1)}, u32[]{:S(2)}) copy-start(bf16[64,4096]{1,0:T(8,128)(2,1)} %param.15) | copy-start | bytes 1572868
  281.2 36.0 %copy-start.9 = (f32[4096]{0:T(1024)S(1)}, f32[4096]{0:T(1024)}, u32[]{:S(2)}) copy-start(f32[4096]{0:T(1024)} %param.24) | copy-start | bytes 49156
  281.2 111.4 %all-gather.8.cloned.1.call-start = ((), (), s32[]{:S(2)}) async-start(), calls=%async_computation.7 | async-start | bytes 4718592 | tf_op jit(solution)/shard_map/all_gather | solution.py:179
  315.6 1.6 copy-start.3
  318.7 194.2 %reduce-scatter.5.cloned.1.call-start = ((), (), s32[]{:S(2)}) async-start(), calls=%async_computation.8 | async-start | bytes 4718592 | tf_op jit(solution)/shard_map/reduce_scatter | solution.py:186
  426.5 0.8 copy-start.8
  426.5 124.8 %all-reduce.9.cloned.1.call-start = ((), (), s32[]{:S(2)}) async-start(), calls=%async_computation.9 | async-start | bytes 2097152 | tf_op jit(solution)/shard_map/psum | solution.py:198
  515.3 38.5 %copy-start.1 = (bf16[1024,1024]{1,0:T(8,128)(2,1)S(1)}, bf16[1024,1024]{1,0:T(8,128)(2,1)}, u32[]{:S(2)}) copy-start(bf16[1024,1024]{1,0:T(8,128)(2,1)} %param.17) | copy-start | bytes 6291460
Sparse Core Ops, SparseCore 0:
  10.1 48.6 all-gather.3
  61.2 34.6 all-reduce.4
  98.2 27.1 reduce-scatter.2
  126.8 148.2 all-gather.5
  281.3 34.2 all-reduce.6
  318.8 73.7 all-gather.7
  426.7 86.1 reduce-scatter.4
  515.5 35.8 all-reduce.8
where the time goes:
time: 561 us
  waiting for transfers between devices  438 us (78%)
  matrix products  51.2 us (9%)
  blocking collectives  42.4 us (8%)
  between operations  13.8 us (2%)
  other arithmetic  11.1 us (2%)
    all_gather x1, waiting for transfers between devices, local(): lax.all_gather(out_weight, 'fsdp', axis=1, tiled=True)  145 us
    reduce_scatter x1, waiting for transfers between devices, local(): lax.psum_scatter(jnp.dot(row_block, down_rows, preferred_element_type=jnp...  85.3 us
    all_gather x1, waiting for transfers between devices, local(): piece_rows = lax.all_gather(send_rows, ('dp', 'fsdp'), axis=0, tiled=True)  73.7 us
    all_gather x1, waiting for transfers between devices, local(): everyone = lax.all_gather(normed, 'fsdp', axis=0, tiled=True)  48.7 us
    psum x1, waiting for transfers between devices, local(): mixture = lax.psum(returned * weight_mine[:, None], 'expert')  36 us
    psum x1, waiting for transfers between devices, local(): residual = window.astype(jnp.float32) + lax.psum(head_terms, 'expert')  34 us
    psum x1, blocking collectives, local(): lax.psum((jnp.dot(columns, key_weight, preferred_element_type=jnp.float32...  23.1 us
    dot_general x1, matrix products, local(): jnp.dot(row_block, down_rows, preferred_element_type=jnp.float32)  21.8 us
  transfers between devices with their start and end apart: 8, of which 7 were waited for; matrix products, arithmetic and copies ran while one was open for 2% of the time, Pallas kernels for 0%

commit v1 on v0

--- a/solution.py
+++ b/solution.py
@@ -8,6 +8,24 @@
 epsilon = 1e-05
 rope_base = 1000000.0
 floor_score = -1e30
+
+
+def joined_along(tiles, dim):
+    dims = list(tiles.shape[1:])
+    dims[dim] *= tiles.shape[0]
+    return jnp.moveaxis(tiles, 0, dim).reshape(dims)
+
+
+def grow_blocks(x, axis):
+    count = lax.axis_size(axis)
+    parts = x[None]
+    for level in range(count.bit_length() - 1):
+        bit = 1 << level
+        other = lax.ppermute(parts, axis, [(i, i ^ bit) for i in range(count)])
+        both = jnp.stack([parts, other])
+        upper = lax.axis_index(axis) >> level & 1
+        parts = jnp.where(upper == 0, both, both[::-1]).reshape(-1, *x.shape)
+    return parts
 
 
 def rms_norm(values, scales):
@@ -77,7 +95,7 @@
     first_row = fsdp_place * token_rows
     own_positions = prefix_rows + first_row + jnp.arange(token_rows, dtype=jnp.int32)
     all_positions = prefix_rows + jnp.arange(window_rows, dtype=jnp.int32)
-    everyone = lax.all_gather(normed, "fsdp", axis=0, tiled=True)
+    everyone = joined_along(grow_blocks(normed, "fsdp"), 0)
     slab_width = query_weight.shape[0]
     columns = lax.dynamic_slice_in_dim(everyone, fsdp_place * slab_width, slab_width, 1)
     row_block = columns

time: 561 us -> 582 us (1.037)
  waiting for transfers between devices: 438 us -> 449 us
    ppermute x0 -> x2, waiting for transfers between devices: none -> 57.3 us  [grow_blocks(): other = lax.ppermute(parts, axis, [(i, i ^ bit) for i in range(count)])]
    all_gather x1 -> x0, waiting for transfers between devices: 48.7 us -> none  [local(): everyone = lax.all_gather(normed, 'fsdp', axis=0, tiled=True)]
    ppermute x0 -> x2, starting transfers between devices: none -> 5.84 us  [grow_blocks(): other = lax.ppermute(parts, axis, [(i, i ^ bit) for i in range(count)])]
  transfers between devices with their start and end apart: 8 -> 9, of which waited for: 7 -> 8; matrix products, arithmetic and copies ran while one was open for 2% -> 2% of each run, Pallas kernels for 0% -> 0%
where the time goes in v1:
time: 582 us
  waiting for transfers between devices  449 us (77%)
  matrix products  50.2 us (9%)
  blocking collectives  43 us (7%)
  other arithmetic  14.6 us (3%)
  between operations  13.8 us (2%)
  starting transfers between devices  6.27 us (1%)
    all_gather x1, waiting for transfers between devices, local(): lax.all_gather(out_weight, 'fsdp', axis=1, tiled=True)  146 us
    reduce_scatter x1, waiting for transfers between devices, local(): lax.psum_scatter(jnp.dot(row_block, down_rows, preferred_element_type=jnp...  85.3 us
    all_gather x1, waiting for transfers between devices, local(): piece_rows = lax.all_gather(send_rows, ('dp', 'fsdp'), axis=0, tiled=True)  73.7 us
    ppermute x2, waiting for transfers between devices, grow_blocks(): other = lax.ppermute(parts, axis, [(i, i ^ bit) for i in range(count)])  57.3 us
    psum x1, waiting for transfers between devices, local(): mixture = lax.psum(returned * weight_mine[:, None], 'expert')  36 us
    psum x1, waiting for transfers between devices, local(): residual = window.astype(jnp.float32) + lax.psum(head_terms, 'expert')  34.1 us
    psum x1, blocking collectives, local(): lax.psum((jnp.dot(columns, key_weight, preferred_element_type=jnp.float32...  24.6 us
    dot_general x1, matrix products, local(): jnp.dot(row_block, down_rows, preferred_element_type=jnp.float32)  21.8 us
  transfers between devices with their start and end apart: 9, of which 8 were waited for; matrix products, arithmetic and copies ran while one was open for 2% of the time, Pallas kernels for 0%

profile of v1, /device:TPU:0, one launch (start us, length us, event | category | flops | bytes accessed | tf_op | source)
XLA Modules:
  0.0 581.6 jit_solution(16294483854638318763)
XLA Ops:
  6.5 1.4 fusion.29
  7.9 1.3 fusion.54
  9.2 3.1 collective-permute-start
  12.3 12.0 %collective-permute-done = bf16[1,64,4096]{2,1,0:T(8,128)(2,1)} collective-permute-done((bf16[1,64,4096]{2,1,0:T(8,128)(2,1)S(1)}, bf16[1,64,4096]{2,1,0:T(8,128)(2,1)}, u32[]{:S(2)}, u32[]{:S(2)}) %collective-permute-start) | collective-permute-done | bytes 524320 | tf_op jit(solution)/shard_map/ppermute | solution.py:24
  24.4 1.1 pad_maximum_fusion.1
  25.5 1.3 fusion.39
  26.8 2.8 collective-permute-start.1
  29.5 45.3 %collective-permute-done.1 = bf16[2,64,4096]{2,1,0:T(8,128)(2,1)} collective-permute-done((bf16[2,64,4096]{2,1,0:T(8,128)(2,1)}, bf16[2,64,4096]{2,1,0:T(8,128)(2,1)}, u32[]{:S(2)}, u32[]{:S(2)}) %collective-permute-start.1) | collective-permute-done | bytes 1048608 | tf_op jit(solution)/shard_map/ppermute | solution.py:24
  74.8 1.4 pad_maximum_fusion
  76.3 0.5 reverse_select_fusion
  76.7 1.4 copy-done.4
  78.1 0.4 fusion.45
  78.5 0.8 copy.41
  79.3 0.0 reduce-scatter.3.cloned.1.call-start
  79.4 2.7 fusion.47
  82.2 0.0 all-gather.3.cloned.1.call-start
  82.2 0.7 all-gather.3.cloned.1.call-update
  82.9 0.0 all-reduce.7.cloned.1.call-start
  83.0 0.1 copy-done.7
  83.1 0.1 copy.37
  83.3 0.1 copy.39
  83.4 4.3 all_gather.15
  87.8 7.0 %all_gather.16 = bf16[1024,256]{0,1:T(8,128)(2,1)S(1)} all-gather(bf16[512,256]{0,1:T(8,128)(2,1)S(1)} %copy.37), channel_id=1, replica_groups=mesh['dp'=2,'fsdp'=4,'expert'=4] {'dp'}, dimensions={0}, use_global_device_ids=true | all-gather | bytes 786432 | tf_op jit(solution)/shard_map/all_gather | solution.py:139
  94.9 7.0 %all_gather.17 = bf16[1024,256]{0,1:T(8,128)(2,1)S(1)} all-gather(bf16[512,256]{0,1:T(8,128)(2,1)S(1)} %copy.39), channel_id=1, replica_groups=mesh['dp'=2,'fsdp'=4,'expert'=4] {'dp'}, dimensions={0}, use_global_device_ids=true | all-gather | bytes 786432 | tf_op jit(solution)/shard_map/all_gather | solution.py:140
  101.9 0.1 iota_compare_fusion
  102.0 0.2 multiply_cosine_fusion.1
  102.2 0.5 multiply_cosine_fusion
  102.8 1.4 fusion.43
  104.1 24.6 %all-reduce.10 = bf16[256,256]{1,0:T(8,128)(2,1)S(1)} all-reduce(f32[256,256]{1,0:T(8,128)S(1)} %fusion.43), channel_id=1, replica_groups=mesh['dp'=2,'fsdp'=4,'expert'=4] {'fsdp'}, use_global_device_ids=true, to_apply=%region_5.6 | all-reduce | flops 65536 | bytes 393216 | tf_op jit(solution)/shard_map/psum | solution.py:108
  128.8 0.0 all-reduce.5.cloned.1.call-done
  128.8 1.2 subtract_convert_fusion
  130.0 15.8 %reduce-scatter.3.cloned.1.call-done = f32[64,1024]{1,0:T(8,128)} async-done(((f32[256,1024]{1,0:T(8,128)}), f32[64,1024]{1,0:T(8,128)}) %reduce-scatter.3.cloned.1.call-update) | async-done | bytes 262160 | tf_op jit(solution)/shard_map/reduce_scatter | solution.py:102
  145.8 1.0 copy.55
  146.8 0.2 subtract_convert_fusion.1
  147.0 0.4 fusion.83
  147.4 0.3 fusion.41
  147.7 0.6 bitcast_reduce_fusion
  148.3 0.6 fusion.20
  149.0 0.6 fusion.27
  149.6 0.3 fusion.28
  149.9 0.1 copy.43
  150.0 0.1 convert_element_type.96
  150.1 145.9 %all-gather.3.cloned.1.call-done = bf16[1024,4096]{1,0:T(8,128)(2,1)} async-done(((bf16[1024,1024]{1,0:T(8,128)(2,1)}), bf16[1024,4096]{1,0:T(8,128)(2,1)}) %all-gather.3.cloned.1.call-update) | async-done | bytes 8388624 | tf_op jit(solution)/shard_map/all_gather | solution.py:168
  296.0 6.0 %fusion.84 = f32[64,4096]{1,0:T(8,128)} fusion(bf16[64,1024]{1,0:T(8,128)(2,1)S(1)} %convert_element_type.96, bf16[1024,4096]{1,0:T(8,128)(2,1)} %all-gather.3.cloned.1.call-done), kind=kOutput, calls=%fused_computation.121 | convolution fusion | flops 536870912 | bytes 9568256 | tf_op jit(solution)/shard_map/dot_general | solution.py:166
  302.1 0.0 all-gather.5.cloned.1.call-start
  302.2 0.1 copy.44
  302.3 0.1 reduce-window.8
  302.4 0.1 reduce.1
  302.5 34.1 %all-reduce.7.cloned.1.call-done = f32[64,4096]{1,0:T(8,128)} async-done(((f32[64,4096]{1,0:T(8,128)}), f32[64,4096]{1,0:T(8,128)}) %all-reduce.7.cloned.1.call-update) | async-done | bytes 1048592 | tf_op jit(solution)/shard_map/psum | solution.py:171
  336.6 1.6 multiply_reduce_fusion
  338.1 0.2 multiply_convert_fusion
  338.3 1.2 convolution_convert_fusion
  339.6 0.0 all-gather.5.cloned.1.call-update
  339.6 0.2 reduce-scatter.5.cloned.1.call-start
  339.8 73.7 %all-gather.5.cloned.1.call-done = bf16[512,4096]{1,0:T(8,128)(2,1)} async-done(((bf16[64,4096]{1,0:T(8,128)(2,1)}), bf16[512,4096]{1,0:T(8,128)(2,1)}) %all-gather.5.cloned.1.call-update) | async-done | bytes 4194320 | tf_op jit(solution)/shard_map/all_gather | solution.py:197
  413.5 12.2 %fusion.4 = f32[512,1536]{1,0:T(8,128)} fusion(bf16[512,4096]{1,0:T(8,128)(2,1)} %all-gather.5.cloned.1.call-done, bf16[1,1536,4096]{2,1,0:T(8,128)(2,1)} %param.27), kind=kOutput, calls=%fused_computation.4 | convolution fusion | flops 6442450944 | bytes 19922944 | tf_op jit(solution)/shard_map/dot_general | solution.py:198
  425.7 21.8 %fusion.6 = bf16[512,4096]{1,0:T(8,128)(2,1)} fusion(bf16[1,1536,4096]{2,1,0:T(8,128)(2,1)} %param.29, bf16[512,4096]{1,0:T(8,128)(2,1)} %all-gather.5.cloned.1.call-done, bf16[1,1536,4096]{2,1,0:T(8,128)(2,1)} %param.28, f32[512,1536]{1,0:T(8,128)} %fusion.4), kind=kOutput, calls=%fused_computation.6 | convolution fusion | flops 12891717632 | bytes 36700160 | tf_op jit(solution)/shard_map/dot_general | solution.py:205
  447.5 0.0 all-reduce.9.cloned.1.call-start
  447.5 0.7 copy-done.9
  448.2 0.2 fusion.85
  448.5 85.3 %reduce-scatter.5.cloned.1.call-done = bf16[64,4096]{1,0:T(8,128)(2,1)} async-done(((bf16[512,4096]{1,0:T(8,128)(2,1)}), bf16[64,4096]{1,0:T(8,128)(2,1)}) %reduce-scatter.5.cloned.1.call-update) | async-done | bytes 524304 | tf_op jit(solution)/shard_map/reduce_scatter | solution.py:204
  533.8 2.4 convolution_multiply_fusion
  536.3 36.0 %all-reduce.9.cloned.1.call-done = f32[64,4096]{1,0:T(8,128)} async-done(((f32[64,4096]{1,0:T(8,128)}), f32[64,4096]{1,0:T(8,128)}) %all-reduce.9.cloned.1.call-update) | async-done | bytes 1048592 | tf_op jit(solution)/shard_map/psum | solution.py:216
  572.3 2.5 fusion.40
  (49 shorter events, 0.4 us)
Async XLA Ops:
  6.5 72.9 %copy-start = (bf16[1024,1024]{1,0:T(8,128)(2,1)S(1)}, bf16[1024,1024]{1,0:T(8,128)(2,1)}, u32[]{:S(2)}) copy-start(bf16[1024,1024]{1,0:T(8,128)(2,1)} %param.17) | copy-start | bytes 6291460
  6.5 122.2 %all-reduce.5.cloned.1.call-start = ((), (), s32[]{:S(2)}) async-start(), calls=%async_computation.3 | async-start | bytes 524288 | tf_op jit(solution)/shard_map/psum | solution.py:108
  9.2 15.1 %collective-permute-start = (bf16[1,64,4096]{2,1,0:T(8,128)(2,1)S(1)}, bf16[1,64,4096]{2,1,0:T(8,128)(2,1)}, u32[]{:S(2)}, u32[]{:S(2)}) collective-permute-start(bf16[1,64,4096]{2,1,0:T(8,128)(2,1)S(1)} %get-tuple-element.11), channel_id=1, source_target_pairs={{0,4},{4,0},{8,12},{12,8},{1,5},{5,1},{9,13},{13,9},{2,6},{6,2},{1... | collective-permute-start | bytes 1572872 | tf_op jit(solution)/shard_map/ppermute | solution.py:24
  26.8 48.0 %collective-permute-start.1 = (bf16[2,64,4096]{2,1,0:T(8,128)(2,1)}, bf16[2,64,4096]{2,1,0:T(8,128)(2,1)}, u32[]{:S(2)}, u32[]{:S(2)}) collective-permute-start(bf16[2,64,4096]{2,1,0:T(8,128)(2,1)} %get-tuple-element.9), channel_id=1, source_target_pairs={{0,8},{4,12},{8,0},{12,4},{1,9},{5,13},{9,1},{13,5},{2,10},{6,14},... | collective-permute-start | bytes 3145736 | tf_op jit(solution)/shard_map/ppermute | solution.py:24
  76.2 1.9 copy-start.5
  76.7 1.4 copy-start.4
  79.3 66.4 %reduce-scatter.3.cloned.1.call-start = ((), (), s32[]{:S(2)}) async-start(), calls=%async_computation.2 | async-start | bytes 1310720 | tf_op jit(solution)/shard_map/reduce_scatter | solution.py:102
  82.1 0.8 copy-start.12
  82.1 1.0 copy-start.7
  82.1 1.1 copy-start.8
  82.2 20.6 %copy-start.6 = (bf16[1024,256]{1,0:T(8,128)(2,1)S(1)}, bf16[1024,256]{1,0:T(8,128)(2,1)}, u32[]{:S(2)}) copy-start(bf16[1024,256]{1,0:T(8,128)(2,1)} %param.19) | copy-start | bytes 1572868
  82.2 213.9 %all-gather.3.cloned.1.call-start = ((), (), s32[]{:S(2)}) async-start(), calls=%async_computation.4 | async-start | bytes 10485760 | tf_op jit(solution)/shard_map/all_gather | solution.py:168
  82.9 253.6 %all-reduce.7.cloned.1.call-start = ((), (), s32[]{:S(2)}) async-start(), calls=%async_computation.5 | async-start | bytes 2097152 | tf_op jit(solution)/shard_map/psum | solution.py:171
  150.1 152.0 %copy-start.11 = (s32[1,64,2]{1,2,0:T(2,128)S(1)}, s32[1,64,2]{1,2,0:T(2,128)}, u32[]{:S(2)}) copy-start(s32[1,64,2]{1,2,0:T(2,128)} %param.26) | copy-start | bytes 1540
  150.1 186.4 %copy-start.2 = (bf16[64,4096]{1,0:T(8,128)(2,1)S(1)}, bf16[64,4096]{1,0:T(8,128)(2,1)}, u32[]{:S(2)}) copy-start(bf16[64,4096]{1,0:T(8,128)(2,1)} %param.15) | copy-start | bytes 1572868
  302.1 36.1 %copy-start.10 = (f32[4096]{0:T(1024)S(1)}, f32[4096]{0:T(1024)}, u32[]{:S(2)}) copy-start(f32[4096]{0:T(1024)} %param.24) | copy-start | bytes 49156
  302.1 111.4 %all-gather.5.cloned.1.call-start = ((), (), s32[]{:S(2)}) async-start(), calls=%async_computation.6 | async-start | bytes 4718592 | tf_op jit(solution)/shard_map/all_gather | solution.py:197
  336.6 1.6 copy-start.3
  339.6 194.2 %reduce-scatter.5.cloned.1.call-start = ((), (), s32[]{:S(2)}) async-start(), calls=%async_computation.7 | async-start | bytes 4718592 | tf_op jit(solution)/shard_map/reduce_scatter | solution.py:204
  447.5 0.8 copy-start.9
  447.5 124.8 %all-reduce.9.cloned.1.call-start = ((), (), s32[]{:S(2)}) async-start(), calls=%async_computation.8 | async-start | bytes 2097152 | tf_op jit(solution)/shard_map/psum | solution.py:216
  536.2 38.5 %copy-start.1 = (bf16[1024,1024]{1,0:T(8,128)(2,1)S(1)}, bf16[1024,1024]{1,0:T(8,128)(2,1)}, u32[]{:S(2)}) copy-start(bf16[1024,1024]{1,0:T(8,128)(2,1)} %param.17) | copy-start | bytes 6291460
Sparse Core Ops, SparseCore 0:
  79.5 36.9 all-reduce.4
  118.9 26.8 reduce-scatter.2
  147.4 148.6 all-gather.2
  302.2 34.2 all-reduce.6
  339.7 73.7 all-gather.4
  447.6 86.1 reduce-scatter.4
  536.4 35.8 all-reduce.8
